TPU v7x, 32 devices: a whole 2x2x4 slice. The times are simulated.
32 devices in a mesh: row: 4 (over y, core), col: 8 (over z, x).
Axes of the slice: x: 2, y: 2, z: 4, core: 2. Of those that a mesh axis runs over, the one named last changes fastest.
Arguments:
- positions: float32 [3, 512], P(None, ('row', 'col')), as said below
- thermal_noise: float32 [32, 3, 512], P(None, None, ('row', 'col')), as said below
Outputs:
- displacement: float32 [32, 3, 512], P(None, None, ('row', 'col'))
Inputs may be any that keep to these rules, and one draw needn't show every extreme that they name: `positions`: any two particles are at least 1.0 apart. `thermal_noise`: finite real entries.
All inputs are finite; a program needn't handle non-finite values.
Results may differ from a plain program's by a relative error of at most 0.0013.
Values may be sent and summed in bfloat16 or wider, within the bound.
A program may use at most 64 MiB of HBM per device.

v0:
```python
import jax
import jax.numpy as jnp
from jax import lax
from jax.sharding import PartitionSpec as P


def pair_tensor(rows_pos, cols_pos, retain):
    offsets = [rows_pos[a][None, :] - cols_pos[a][:, None] for a in range(3)]
    squared = offsets[0] * offsets[0] + offsets[1] * offsets[1] + offsets[2] * offsets[2]
    guarded = jnp.where(retain, squared, 4.0)
    inverse = lax.rsqrt(guarded)
    distance = guarded * inverse
    correlation = distance < 2.0
    inverse_cube = inverse * inverse * inverse
    inverse_fifth = inverse_cube * inverse * inverse
    isotropic = jnp.where(
        correlation, 1.0 - 0.28125 * distance, 0.75 * inverse + 0.5 * inverse_cube
    )
    dyadic = jnp.where(correlation, 0.09375 * inverse, 0.75 * inverse_cube - 1.5 * inverse_fifth)
    isotropic = jnp.where(retain, isotropic, 0.0)
    dyadic = jnp.where(retain, dyadic, 0.0)
    columns = []
    for b in range(3):
        elements = []
        for a in range(3):
            element = dyadic * offsets[a] * offsets[b]
            if a == b:
                element = element + isotropic
            elements.append(element)
        columns.append(jnp.stack(elements, axis=1))
    return jnp.stack(columns, axis=0)


def half_image(pos_rows, pos_cols, vec_rows, vec_cols, own_vector):
    row_devices = lax.axis_size("row")
    col_devices = lax.axis_size("col")
    row_index = lax.axis_index("row")
    col_index = lax.axis_index("col")
    samples = own_vector.shape[0]
    per_device = own_vector.shape[2]
    row_count = pos_rows.shape[1]
    row_label = row_index * col_devices * per_device + lax.iota(jnp.int32, row_count)
    group_size = min(row_devices, max(1, 128 // per_device))
    width = group_size * per_device
    group_count = row_devices // group_size
    sum_rows = jnp.zeros((samples, 3, row_count), jnp.float32)
    sum_cols = jnp.zeros((samples, 3, per_device * row_devices), jnp.float32)

    def add_group(group, totals):
        sum_rows, sum_cols = totals
        start = group * width
        cols_pos = lax.dynamic_slice_in_dim(pos_cols, start, width, 1)
        cols_vec = lax.dynamic_slice_in_dim(vec_cols, start, width, 2)
        local_cols = lax.iota(jnp.int32, width)
        segment = group * group_size + local_cols // per_device
        col_label = (segment * col_devices + col_index) * per_device + local_cols % per_device
        keep = segment >= row_index
        upper = (segment != row_index)[:, None] | (row_label[None, :] < col_label[:, None])
        retain = keep[:, None] & upper & (row_label[None, :] != col_label[:, None])
        tensor = pair_tensor(pos_rows, cols_pos, retain).astype(jnp.bfloat16)
        sum_rows = sum_rows + jnp.einsum(
            "kbj,bjai->kai", cols_vec, tensor, preferred_element_type=jnp.float32
        )
        credit = jnp.einsum("kai,bjai->kbj", vec_rows, tensor, preferred_element_type=jnp.float32)
        previous = lax.dynamic_slice_in_dim(sum_cols, start, width, 2)
        sum_cols = lax.dynamic_update_slice_in_dim(sum_cols, previous + credit, start, 2)
        return (sum_rows, sum_cols)

    totals = (sum_rows, sum_cols)
    totals = lax.fori_loop(row_index // group_size, group_count, add_group, totals)
    sum_rows, sum_cols = totals
    mobility_image = own_vector + lax.psum_scatter(sum_rows, "col", scatter_dimension=2, tiled=True)
    return mobility_image + lax.psum_scatter(sum_cols, "row", scatter_dimension=2, tiled=True)


def on_device(positions, thermal_noise):
    squares = lax.psum(jnp.sum(thermal_noise * thermal_noise, axis=(1, 2)), ("row", "col"))
    noise_length = jnp.sqrt(squares + 1e-06)
    basis_one = thermal_noise / noise_length[:, None, None]
    pos_cols, cols_one = (
        lax.all_gather(positions, "row", axis=1, tiled=True),
        lax.all_gather(basis_one, "row", axis=2, tiled=True),
    )
    pos_rows, rows_wide = (
        lax.all_gather(positions, "col", axis=1, tiled=True),
        lax.all_gather(basis_one, "col", axis=2, tiled=True),
    )
    image_one = half_image(
        pos_rows, pos_cols, rows_wide.astype(jnp.bfloat16), cols_one.astype(jnp.bfloat16), basis_one
    )
    alpha_one = lax.psum(jnp.sum(basis_one * image_one, axis=(1, 2)), ("row", "col"))
    remainder = image_one - alpha_one[:, None, None] * basis_one
    beta_squared = lax.psum(jnp.sum(remainder * remainder, axis=(1, 2)), ("row", "col"))
    beta_one = jnp.sqrt(beta_squared + 1e-06)
    basis_two = remainder / beta_one[:, None, None]
    narrow_two = basis_two.astype(jnp.bfloat16)
    cols_two = lax.all_gather(narrow_two, "row", axis=2, tiled=True)
    rows_two = lax.all_gather(narrow_two, "col", axis=2, tiled=True)
    image_two = half_image(pos_rows, pos_cols, rows_two, cols_two, basis_two)
    alpha_two = lax.psum(jnp.sum(basis_two * image_two, axis=(1, 2)), ("row", "col"))
    det_root = jnp.sqrt(alpha_one * alpha_two - beta_one * beta_one)
    trace_root = jnp.sqrt(alpha_one + alpha_two + 2.0 * det_root)
    weight_one = (alpha_one + det_root) / trace_root
    weight_two = beta_one / trace_root
    return (
        0.5
        * noise_length[:, None, None]
        * (weight_one[:, None, None] * basis_one + weight_two[:, None, None] * basis_two)
    )


def solution(mesh):
    return jax.shard_map(
        on_device,
        mesh=mesh,
        in_specs=(P(None, ("row", "col")), P(None, None, ("row", "col"))),
        out_specs=P(None, None, ("row", "col")),
        check_vma=False,
    )
```

profile of v0, /device:TPU:0, one launch (start us, length us, event | category | flops | bytes accessed | tf_op | source)
XLA Modules:
  0.0 451.7 jit_solution(3374881495807771110)
XLA Ops:
  6.5 0.0 reduce-scatter.7.cloned.1.call-start
  6.5 0.0 copy-start.3
  6.5 0.7 copy-done.3
  7.2 28.1 %all-gather = f32[8,16,3]{1,2,0:T(4,128)S(1)} all-gather(f32[1,16,3]{1,2,0:T(4,128)S(1)} %bitcast.133), channel_id=1, replica_groups=mesh['row'=4,'col'=8] {'col'}, dimensions={0}, use_global_device_ids=true | all-gather | bytes 1728 | tf_op jit(solution)/shard_map/all_gather | solution.py:85
  35.3 5.2 %all-gather.1 = f32[4,16,3]{1,2,0:T(4,128)S(1)} all-gather(f32[1,16,3]{1,2,0:T(4,128)S(1)} %bitcast.134), channel_id=1, replica_groups=mesh['row'=4,'col'=8] {'row'}, dimensions={0}, use_global_device_ids=true | all-gather | bytes 960 | tf_op jit(solution)/shard_map/all_gather | solution.py:81
  40.5 0.0 copy-done
  40.5 38.9 %psum.28 = f32[32]{0:T(128)S(1)} all-reduce(f32[32]{0:T(128)S(1)} %multiply_reduce_fusion.3), channel_id=1, replica_groups=mesh['row'=4,'col'=8] {'row','col'}, use_global_device_ids=true, to_apply=%region_1.0 | all-reduce | flops 32 | bytes 256 | tf_op jit(solution)/shard_map/psum | solution.py:77
  79.5 5.5 %all_gather.20 = bf16[32,3,64]{0,2,1:T(8,128)(2,1)S(1)} all-gather(bf16[32,3,16]{0,2,1:T(8,128)(2,1)S(1)} %convert.110), channel_id=1, replica_groups=mesh['row'=4,'col'=8] {'row'}, dimensions={2}, use_global_device_ids=true | all-gather | bytes 15360 | tf_op jit(solution)/shard_map/all_gather | solution.py:82
  85.0 0.1 copy.39
  85.1 30.6 %all_gather.21 = bf16[32,3,128]{0,2,1:T(8,128)(2,1)S(1)} all-gather(bf16[32,3,16]{0,2,1:T(8,128)(2,1)S(1)} %get-tuple-element.415), channel_id=1, replica_groups=mesh['row'=4,'col'=8] {'col'}, dimensions={2}, use_global_device_ids=true | all-gather | bytes 27648 | tf_op jit(solution)/shard_map/all_gather | solution.py:86
  115.6 0.1 copy.40
  115.7 0.1 reshape.5452
  115.8 0.1 reshape.5454
  115.9 0.7 while.30
  116.0 0.2 fusion.88
  116.3 0.2 fusion.90
  116.4 0.2 fusion.89
  116.6 0.7 copy.42
  117.4 0.0 reduce-scatter.7.cloned.1.call-update
  117.4 0.0 reduce-scatter.5.cloned.1.call-start
  117.5 0.8 copy.41
  118.3 0.0 reduce-scatter.5.cloned.1.call-update
  118.3 0.0 reduce-scatter.11.cloned.1.call-start
  118.3 17.6 %reduce-scatter.7.cloned.1.call-done = f32[32,3,16]{0,2,1:T(8,128)} async-done(((f32[32,3,64]{0,2,1:T(8,128)}), f32[32,3,16]{0,2,1:T(8,128)}) %reduce-scatter.7.cloned.1.call-update) | async-done | bytes 6160 | tf_op jit(solution)/shard_map/reduce_scatter | solution.py:73
  135.9 65.3 %reduce-scatter.5.cloned.1.call-done = f32[32,3,16]{0,2,1:T(8,128)} async-done(((f32[32,3,128]{0,2,1:T(8,128)}), f32[32,3,16]{0,2,1:T(8,128)}) %reduce-scatter.5.cloned.1.call-update) | async-done | bytes 6160 | tf_op jit(solution)/shard_map/reduce_scatter | solution.py:72
  201.2 0.8 multiply_reduce_fusion.2
  202.1 40.1 %psum.29 = f32[32]{0:T(128)S(1)} all-reduce(f32[32]{0:T(128)S(1)} %multiply_reduce_fusion.2), channel_id=1, replica_groups=mesh['row'=4,'col'=8] {'row','col'}, use_global_device_ids=true, to_apply=%region_7.8 | all-reduce | flops 32 | bytes 256 | tf_op jit(solution)/shard_map/psum | solution.py:91
  242.2 0.0 copy-done.1
  242.2 0.0 copy-done.2
  242.2 39.1 %psum.30 = f32[32]{0:T(128)S(1)} all-reduce(f32[32]{0:T(128)S(1)} %get-tuple-element.413), channel_id=1, replica_groups=mesh['row'=4,'col'=8] {'row','col'}, use_global_device_ids=true, to_apply=%region_9.10 | all-reduce | flops 32 | bytes 256 | tf_op jit(solution)/shard_map/psum | solution.py:93
  281.3 30.5 %all_gather.23 = bf16[32,3,128]{0,2,1:T(8,128)(2,1)S(1)} all-gather(bf16[32,3,16]{0,2,1:T(8,128)(2,1)S(1)} %fusion.71), channel_id=1, replica_groups=mesh['row'=4,'col'=8] {'col'}, dimensions={2}, use_global_device_ids=true | all-gather | bytes 27648 | tf_op jit(solution)/shard_map/all_gather | solution.py:98
  311.9 5.5 %all_gather.22 = bf16[32,3,64]{0,2,1:T(8,128)(2,1)S(1)} all-gather(bf16[32,3,16]{0,2,1:T(8,128)(2,1)S(1)} %fusion.71), channel_id=1, replica_groups=mesh['row'=4,'col'=8] {'row'}, dimensions={2}, use_global_device_ids=true | all-gather | bytes 15360 | tf_op jit(solution)/shard_map/all_gather | solution.py:97
  317.4 0.1 copy.44
  317.5 0.1 copy.43
  317.6 0.7 while.31
  317.7 0.2 fusion.94
  318.0 0.2 fusion.96
  318.2 0.2 fusion.95
  318.4 0.7 copy.46
  319.1 0.0 reduce-scatter.11.cloned.1.call-update
  319.1 0.0 reduce-scatter.9.cloned.1.call-start
  319.2 0.8 copy.45
  320.0 0.0 reduce-scatter.9.cloned.1.call-update
  320.0 18.4 %reduce-scatter.11.cloned.1.call-done = f32[32,3,16]{0,2,1:T(8,128)} async-done(((f32[32,3,64]{0,2,1:T(8,128)}), f32[32,3,16]{0,2,1:T(8,128)}) %reduce-scatter.11.cloned.1.call-update) | async-done | bytes 6160 | tf_op jit(solution)/shard_map/reduce_scatter | solution.py:73
  338.4 65.2 %reduce-scatter.9.cloned.1.call-done = f32[32,3,16]{0,2,1:T(8,128)} async-done(((f32[32,3,128]{0,2,1:T(8,128)}), f32[32,3,16]{0,2,1:T(8,128)}) %reduce-scatter.9.cloned.1.call-update) | async-done | bytes 6160 | tf_op jit(solution)/shard_map/reduce_scatter | solution.py:72
  403.6 0.8 multiply_reduce_fusion
  404.4 40.2 %psum.31 = f32[32]{0:T(128)S(1)} all-reduce(f32[32]{0:T(128)S(1)} %multiply_reduce_fusion), channel_id=1, replica_groups=mesh['row'=4,'col'=8] {'row','col'}, use_global_device_ids=true, to_apply=%region_15.16 | all-reduce | flops 32 | bytes 256 | tf_op jit(solution)/shard_map/psum | solution.py:100
  444.6 0.6 add_multiply_fusion
  (33 shorter events, 0.3 us)
Async XLA Ops:
  6.5 129.4 %reduce-scatter.7.cloned.1.call-start = ((), (), s32[]{:S(2)}) async-start(), calls=%async_computation.5 | async-start | bytes 122880 | tf_op jit(solution)/shard_map/reduce_scatter | solution.py:73
  6.5 0.7 copy-start.3
  7.2 33.2 %copy-start = (f32[32,3,16]{0,2,1:T(8,128)S(1)}, f32[32,3,16]{0,2,1:T(8,128)}, u32[]{:S(2)}) copy-start(f32[32,3,16]{0,2,1:T(8,128)} %param.7) | copy-start | bytes 18436
  117.4 83.8 %reduce-scatter.5.cloned.1.call-start = ((), (), s32[]{:S(2)}) async-start(), calls=%async_computation.4 | async-start | bytes 221184 | tf_op jit(solution)/shard_map/reduce_scatter | solution.py:72
  118.3 220.2 %reduce-scatter.11.cloned.1.call-start = ((), (), s32[]{:S(2)}) async-start(), calls=%async_computation.7 | async-start | bytes 122880 | tf_op jit(solution)/shard_map/reduce_scatter | solution.py:73
  135.9 106.2 %copy-start.1 = (f32[32,3,16]{0,2,1:T(8,128)S(1)}, f32[32,3,16]{0,2,1:T(8,128)}, u32[]{:S(2)}) copy-start(f32[32,3,16]{0,2,1:T(8,128)} %reduce-scatter.7.cloned.1.call-done) | copy-start | bytes 18436
  201.2 40.9 %copy-start.2 = (f32[32,3,16]{0,2,1:T(8,128)S(1)}, f32[32,3,16]{0,2,1:T(8,128)}, u32[]{:S(2)}) copy-start(f32[32,3,16]{0,2,1:T(8,128)} %reduce-scatter.5.cloned.1.call-done) | copy-start | bytes 18436
  319.1 84.5 %reduce-scatter.9.cloned.1.call-start = ((), (), s32[]{:S(2)}) async-start(), calls=%async_computation.6 | async-start | bytes 221184 | tf_op jit(solution)/shard_map/reduce_scatter | solution.py:72
Sparse Core Ops, SparseCore 0:
  117.5 18.3 reduce-scatter.6
  139.2 61.9 reduce-scatter.4
  319.2 19.1 reduce-scatter.10
  341.6 61.9 reduce-scatter.8
where the time goes:
time: 453 us; the launch traced here: 452 us
  blocking collectives  264 us (58%)
  waiting for transfers between devices  167 us (37%)
  between operations  13.2 us (3%)
    reduce_scatter x2, waiting for transfers between devices, half_image(): lax.psum_scatter(sum_rows, 'col', scatter_dimension=2, tiled=True)  130 us
    psum x1, blocking collectives, on_device(): lax.psum(jnp.sum(basis_two * image_two, axis=(1, 2)), ('row', 'col'))  40.2 us
    psum x1, blocking collectives, on_device(): lax.psum(jnp.sum(basis_one * image_one, axis=(1, 2)), ('row', 'col'))  40.1 us
    psum x1, blocking collectives, on_device(): lax.psum(jnp.sum(remainder * remainder, axis=(1, 2)), ('row', 'col'))  39.1 us
    psum x1, blocking collectives, on_device(): lax.psum(jnp.sum(thermal_noise * thermal_noise, axis=(1, 2)), ('row', 'co...  38.9 us
    reduce_scatter x2, waiting for transfers between devices, half_image(): lax.psum_scatter(sum_cols, 'row', scatter_dimension=2, tiled=True)  36 us
    all_gather x1, blocking collectives, on_device(): lax.all_gather(basis_one, 'col', axis=2, tiled=True)  30.6 us
    all_gather x1, blocking collectives, on_device(): rows_two = lax.all_gather(narrow_two, 'col', axis=2, tiled=True)  30.5 us
  transfers between devices with their start and end apart: 4, of which 4 were waited for; matrix products, arithmetic and copies ran while one was open for 0% of the time, Pallas kernels for 0%

commit v1 on v0

--- a/solution.py
+++ b/solution.py
@@ -1,7 +1,244 @@
+import functools
+
 import jax
 import jax.numpy as jnp
 from jax import lax
+from jax.experimental import pallas as pl
+from jax.experimental.pallas import tpu as pltpu
 from jax.sharding import PartitionSpec as P
+
+LANES = 128
+MESH = pl.DeviceIdType.MESH
+BLOCKS = ((0, 0), (1, 1), (2, 2), (0, 1), (0, 2), (1, 2))
+
+
+def replicated_kernel(
+    rows,
+    cols,
+    noise_ref,
+    pos_ref,
+    out_ref,
+    gathered,
+    stage,
+    own_ref,
+    noise_full,
+    pos_cols,
+    pos_rows,
+    mobility,
+    weights,
+    image,
+    send_col,
+    recv_col,
+    send_row,
+    recv_row,
+):
+    _, per_device, samples = noise_ref.shape
+    particles = rows * cols * per_device
+    f32, bf16 = jnp.float32, jnp.bfloat16
+    my_row, my_col = lax.axis_index("row"), lax.axis_index("col")
+
+    col_peers = [lax.rem(my_col + k, cols) for k in range(1, cols)]
+    row_peers = [lax.rem(my_row + k, rows) for k in range(1, rows)]
+
+    barrier = pltpu.get_barrier_semaphore()
+    for peer in col_peers:
+        pl.semaphore_signal(barrier, inc=1, device_id=(my_row, peer), device_id_type=MESH)
+    for peer in row_peers:
+        pl.semaphore_signal(barrier, inc=1, device_id=(peer, my_col), device_id_type=MESH)
+
+    stage[...] = jnp.zeros_like(stage)
+    position = pos_ref[...]
+    for term in range(3):
+        piece = position.astype(bf16).astype(f32)
+        stage[pl.ds(3 * term, 3), pl.ds(0, per_device)] = piece
+        position = position - piece
+    turned = jnp.transpose(stage[...])
+    own_ref[...] = jnp.zeros_like(own_ref)
+    for b in range(3):
+        own_ref[:, pl.ds(b * samples, samples)] = noise_ref[b]
+    own_ref[:, pl.ds(3 * samples, 16)] = turned[0:per_device, :]
+    own = own_ref[...]
+    gathered[my_row, my_col] = own.astype(bf16)
+
+    pl.semaphore_wait(barrier, cols + rows - 2)
+
+    def col_copy(peer, source):
+        return pltpu.make_async_remote_copy(
+            src_ref=gathered.at[my_row, my_col],
+            dst_ref=gathered.at[my_row, my_col],
+            send_sem=send_col.at[peer],
+            recv_sem=recv_col.at[source],
+            device_id=(my_row, peer),
+            device_id_type=MESH,
+        )
+
+    def row_copy(block, peer):
+        return pltpu.make_async_remote_copy(
+            src_ref=gathered.at[my_row, block],
+            dst_ref=gathered.at[my_row, block],
+            send_sem=send_row.at[peer],
+            recv_sem=recv_row.at[my_row],
+            device_id=(peer, my_col),
+            device_id_type=MESH,
+        )
+
+    for peer in col_peers:
+        col_copy(peer, my_col).start()
+    for peer in row_peers:
+        row_copy(my_col, peer).start()
+    for k in range(1, cols):
+        source = lax.rem(my_col + cols - k, cols)
+        pltpu.make_async_copy(
+            gathered.at[my_row, source], gathered.at[my_row, source], recv_col.at[source]
+        ).wait()
+        for peer in row_peers:
+            row_copy(source, peer).start()
+    for peer in row_peers:
+        pltpu.make_async_copy(gathered.at[peer], gathered.at[peer], recv_row.at[peer]).wait()
+
+    packed = gathered[...].reshape(particles, LANES)
+    lane = lax.broadcasted_iota(jnp.int32, (1, LANES), 1)
+    field = lax.broadcasted_iota(jnp.int32, (LANES, 3 * LANES), 0) - 3 * samples
+    target = lax.broadcasted_iota(jnp.int32, (LANES, 3 * LANES), 1) // LANES
+    select = (field == target) | (field == target + 3) | (field == target + 6)
+    pos_cols[...] = jnp.dot(packed, select.astype(f32).astype(bf16), preferred_element_type=f32)
+    field = lax.broadcasted_iota(jnp.int32, (3 * 16, LANES), 1) - 3 * samples
+    target = lax.broadcasted_iota(jnp.int32, (3 * 16, LANES), 0) // 16
+    select = (field == target) | (field == target + 3) | (field == target + 6)
+    pos_rows[...] = lax.dot_general(
+        select.astype(f32).astype(bf16), packed, (((1,), (1,)), ((), ())), preferred_element_type=f32
+    )
+
+    @pl.loop(0, particles // 16)
+    def _(step):
+        start = pl.multiple_of(step * 16, 16)
+        at_rows = pl.ds(start, 16)
+        row_pos = [pos_cols[at_rows, pl.ds(a * LANES, LANES)] for a in range(3)]
+        row_label = start + lax.broadcasted_iota(jnp.int32, (16, LANES), 0)
+        for tile in range(particles // LANES):
+            at_cols = pl.ds(tile * LANES, LANES)
+            d = [row_pos[a] - pos_rows[pl.ds(a * 16, 16), at_cols] for a in range(3)]
+            col_label = tile * LANES + lax.broadcasted_iota(jnp.int32, (16, LANES), 1)
+            retain = row_label != col_label
+            q = jnp.where(retain, d[0] * d[0] + d[1] * d[1] + d[2] * d[2], 4.0)
+            u = lax.rsqrt(q)
+            r = q * u
+            near = r < 2.0
+            u2 = u * u
+            f = jnp.where(near, 1.0 - 0.28125 * r, u * (0.75 + 0.5 * u2))
+            f = jnp.where(retain, f, 0.0)
+            h = u * jnp.where(near, 0.09375, u2 * (0.75 - 1.5 * u2))
+            hd = [h * d[a] for a in range(3)]
+            for n, (a, b) in enumerate(BLOCKS):
+                element = hd[a] * d[b]
+                if a == b:
+                    element = element + f
+                mobility[at_rows, pl.ds(n * particles + tile * LANES, LANES)] = element.astype(bf16)
+
+    def set_weights(x):
+        down = pltpu.roll(x, LANES - samples, 1)
+        up = pltpu.roll(x, samples, 1)
+        across = pltpu.roll(x, 2 * samples, 1)
+        group = lane // samples
+        moved = {
+            (0, 0): jnp.where(group == 0, x, 0.0),
+            (1, 1): jnp.where(group == 1, x, 0.0),
+            (2, 2): jnp.where(group == 2, x, 0.0),
+            (0, 1): jnp.where(group == 0, down, jnp.where(group == 1, up, 0.0)),
+            (1, 2): jnp.where(group == 1, down, jnp.where(group == 2, up, 0.0)),
+            (0, 2): jnp.where((group == 0) | (group == 2), across, 0.0),
+        }
+        for n, pair in enumerate(BLOCKS):
+            weights[pl.ds(n * particles, particles), :] = moved[pair].astype(bf16)
+
+    def total(x):
+        column = jnp.sum(x, axis=0, keepdims=True)
+        column = jnp.broadcast_to(column, (8, LANES))
+        column = column + pltpu.roll(column, 2 * samples, 1)
+        column = column + pltpu.roll(column, samples, 1)
+        return column[0:1, :]
+
+    is_noise = lane < 3 * samples
+    me = pl.multiple_of((my_row * cols + my_col) * per_device, per_device)
+    at_own = pl.ds(me, per_device)
+    wide = packed.astype(f32)
+    set_weights(wide)
+    noise_full[...] = jnp.where(is_noise, wide, 0.0)
+    noise_full[at_own, :] = jnp.where(is_noise, own_ref[...], 0.0)
+
+    noise = noise_full[...]
+    length = jnp.sqrt(total(noise * noise) + 1e-06)
+    inverse = 1.0 / length
+    coupled = jnp.dot(mobility[...], weights[...], preferred_element_type=f32)
+    basis_one = noise * inverse
+    image_one = basis_one + coupled * inverse
+    alpha_one = total(basis_one * image_one)
+    remainder = image_one - alpha_one * basis_one
+    beta_one = jnp.sqrt(total(remainder * remainder) + 1e-06)
+    basis_two = remainder * (1.0 / beta_one)
+    image[...] = basis_two
+    set_weights(basis_two)
+    coupled = jnp.dot(mobility[...], weights[...], preferred_element_type=f32)
+    basis_two = image[...]
+    alpha_two = total(basis_two * (basis_two + coupled))
+    det_root = jnp.sqrt(alpha_one * alpha_two - beta_one * beta_one)
+    trace_root = jnp.sqrt(alpha_one + alpha_two + 2.0 * det_root)
+    weight_one = (alpha_one + det_root) / trace_root
+    weight_two = beta_one / trace_root
+    own_one = noise_full[at_own, :] * inverse
+    own_two = image[at_own, :]
+    result = 0.5 * length * (weight_one * own_one + weight_two * own_two)
+    for b in range(3):
+        out_ref[b] = result[:, b * samples : (b + 1) * samples]
+
+    for peer in col_peers:
+        col_copy(peer, my_col).wait_send()
+    for peer in row_peers:
+        pltpu.make_async_copy(gathered.at[my_row], gathered.at[my_row], send_row.at[peer]).wait()
+
+
+def replicated(mesh, positions, thermal_noise):
+    rows, cols = mesh.shape["row"], mesh.shape["col"]
+    samples, _, per_device = thermal_noise.shape
+    particles = rows * cols * per_device
+    f32, bf16 = jnp.float32, jnp.bfloat16
+    vmem = pl.BlockSpec(memory_space=pltpu.VMEM)
+    out = pl.pallas_call(
+        functools.partial(replicated_kernel, rows, cols),
+        out_shape=jax.ShapeDtypeStruct((3, per_device, samples), f32),
+        in_specs=[vmem, vmem],
+        out_specs=vmem,
+        scratch_shapes=[
+            pltpu.VMEM((rows, cols, per_device, LANES), bf16),
+            pltpu.VMEM((16, LANES), f32),
+            pltpu.VMEM((per_device, LANES), f32),
+            pltpu.VMEM((particles, LANES), f32),
+            pltpu.VMEM((particles, 3 * LANES), f32),
+            pltpu.VMEM((3 * 16, particles), f32),
+            pltpu.VMEM((particles, 6 * particles), bf16),
+            pltpu.VMEM((6 * particles, LANES), bf16),
+            pltpu.VMEM((particles, LANES), f32),
+            pltpu.SemaphoreType.DMA((cols,)),
+            pltpu.SemaphoreType.DMA((cols,)),
+            pltpu.SemaphoreType.DMA((rows,)),
+            pltpu.SemaphoreType.DMA((rows,)),
+        ],
+        compiler_params=pltpu.CompilerParams(collective_id=0, has_side_effects=True),
+        name="lanczos",
+    )(jnp.transpose(thermal_noise, (1, 2, 0)), positions)
+    return jnp.transpose(out, (2, 0, 1))
+
+
+def fits(mesh, positions, thermal_noise):
+    devices = mesh.shape["row"] * mesh.shape["col"]
+    samples, _, particles = thermal_noise.shape
+    per_device = particles // devices
+    return (
+        4 * samples == LANES
+        and per_device % 16 == 0
+        and particles % LANES == 0
+        and 12 * particles * particles <= 2**24
+    )
 
 
 def pair_tensor(rows_pos, cols_pos, retain):
@@ -110,10 +347,18 @@
 
 
 def solution(mesh):
-    return jax.shard_map(
-        on_device,
+    specs = dict(
         mesh=mesh,
         in_specs=(P(None, ("row", "col")), P(None, None, ("row", "col"))),
         out_specs=P(None, None, ("row", "col")),
         check_vma=False,
     )
+
+    def program(positions, thermal_noise):
+        if fits(mesh, positions, thermal_noise):
+            body = functools.partial(replicated, mesh)
+        else:
+            body = on_device
+        return jax.shard_map(body, **specs)(positions, thermal_noise)
+
+    return program

time: 453 us -> 21.5 us (0.05)
  blocking collectives: 264 us -> 0 us
  waiting for transfers between devices: 167 us -> 0 us
  Pallas kernels: 0 us -> 19.9 us
  between operations: 13.2 us -> 0.01 us
    reduce_scatter x4 -> x0, waiting for transfers between devices: 166 us -> none  [the longest x2 130 us: half_image(): lax.psum_scatter(sum_rows, 'col', scatter_dimension=2, tiled=True)]
    psum x4 -> x0, blocking collectives: 158 us -> none  [the longest x1 40.2 us: on_device(): lax.psum(jnp.sum(basis_two * image_two, axis=(1, 2)), ('row', 'col'))]
    all_gather x6 -> x0, blocking collectives: 105 us -> none  [the longest x1 30.6 us: on_device(): lax.all_gather(basis_one, 'col', axis=2, tiled=True)]
    pallas_call x0 -> x1, Pallas kernels: none -> 19.9 us  [replicated(): pl.pallas_call(functools.partial(replicated_kernel, rows, cols), out_shap...]
  transfers between devices with their start and end apart: 4 -> 0, of which waited for: 4 -> 0; matrix products, arithmetic and copies ran while one was open for 0% -> 0% of each run, Pallas kernels for 0% -> 0%
where the time goes in v1:
time: 21.5 us; the launch traced here: 21.2 us
  Pallas kernels  19.9 us (93%)
  local copies, waits for them, and re-layouts  1.35 us (6%)
    pallas_call x1, Pallas kernels, replicated(): pl.pallas_call(functools.partial(replicated_kernel, rows, cols), out_shap...  19.9 us
    unnamed x1, local copies, waits for them, and re-layouts  1.35 us

profile of v1, /device:TPU:0, one launch (start us, length us, event | category | flops | bytes accessed | tf_op | source)
XLA Modules:
  0.0 21.2 jit_solution(10150456801774452439)
XLA Ops:
  0.0 19.9 %lanczos.1 = f32[3,16,32]{2,1,0:T(8,128)} custom-call(f32[3,16,32]{2,1,0:T(8,128)} %bitcast.3, f32[3,16]{1,0:T(4,128)} %pos_ref.1), custom_call_target="tpu_custom_call" | custom-call | tf_op jit(solution)/shard_map/lanczos/pallas_call | solution.py:206
  19.9 1.3 %copy.4 = f32[32,3,16]{0,2,1:T(8,128)} copy(f32[32,3,16]{0,2,1:T(8,128)} %bitcast.2) | data formatting | bytes 12288

commit v2 on v1

--- a/solution.py
+++ b/solution.py
@@ -12,9 +12,22 @@
 BLOCKS = ((0, 0), (1, 1), (2, 2), (0, 1), (0, 2), (1, 2))
 
 
+def partner(place, k, size):
+    if size & (size - 1):
+        return lax.rem(place + k, size)
+    result = 0
+    bit = 1
+    while bit < size:
+        digit = lax.rem(place // bit, 2)
+        result = result + bit * (1 - digit if k & bit else digit)
+        bit = 2 * bit
+    return result
+
+
 def replicated_kernel(
     rows,
-    cols,
+    outer,
+    inner,
     noise_ref,
     pos_ref,
     out_ref,
@@ -27,24 +40,34 @@
     mobility,
     weights,
     image,
-    send_col,
-    recv_col,
-    send_row,
-    recv_row,
+    send_line,
+    recv_line,
+    send_plane,
+    recv_plane,
 ):
     _, per_device, samples = noise_ref.shape
-    particles = rows * cols * per_device
+    particles = rows * outer * inner * per_device
     f32, bf16 = jnp.float32, jnp.bfloat16
     my_row, my_col = lax.axis_index("row"), lax.axis_index("col")
 
-    col_peers = [lax.rem(my_col + k, cols) for k in range(1, cols)]
-    row_peers = [lax.rem(my_row + k, rows) for k in range(1, rows)]
+    my_outer, my_inner = my_col // inner, lax.rem(my_col, inner)
+    line = [partner(my_outer, k, outer) for k in range(1, outer)]
+    plane = [
+        (partner(my_row, j, rows), partner(my_inner, i, inner))
+        for i in range(inner)
+        for j in range(rows)
+        if i or j
+    ]
 
     barrier = pltpu.get_barrier_semaphore()
-    for peer in col_peers:
-        pl.semaphore_signal(barrier, inc=1, device_id=(my_row, peer), device_id_type=MESH)
-    for peer in row_peers:
-        pl.semaphore_signal(barrier, inc=1, device_id=(peer, my_col), device_id_type=MESH)
+    for place in line:
+        pl.semaphore_signal(
+            barrier, inc=1, device_id=(my_row, place * inner + my_inner), device_id_type=MESH
+        )
+    for row, place in plane:
+        pl.semaphore_signal(
+            barrier, inc=1, device_id=(row, my_outer * inner + place), device_id_type=MESH
+        )
 
     stage[...] = jnp.zeros_like(stage)
     position = pos_ref[...]
@@ -58,43 +81,43 @@
         own_ref[:, pl.ds(b * samples, samples)] = noise_ref[b]
     own_ref[:, pl.ds(3 * samples, 16)] = turned[0:per_device, :]
     own = own_ref[...]
-    gathered[my_row, my_col] = own.astype(bf16)
-
-    pl.semaphore_wait(barrier, cols + rows - 2)
-
-    def col_copy(peer, source):
+    gathered[my_row, my_inner, my_outer] = own.astype(bf16)
+
+    pl.semaphore_wait(barrier, len(line) + len(plane))
+
+    def line_copy(place, source):
         return pltpu.make_async_remote_copy(
-            src_ref=gathered.at[my_row, my_col],
-            dst_ref=gathered.at[my_row, my_col],
-            send_sem=send_col.at[peer],
-            recv_sem=recv_col.at[source],
-            device_id=(my_row, peer),
+            src_ref=gathered.at[my_row, my_inner, my_outer],
+            dst_ref=gathered.at[my_row, my_inner, my_outer],
+            send_sem=send_line.at[place],
+            recv_sem=recv_line.at[source],
+            device_id=(my_row, place * inner + my_inner),
             device_id_type=MESH,
         )
 
-    def row_copy(block, peer):
+    def plane_copy(block, row, place):
         return pltpu.make_async_remote_copy(
-            src_ref=gathered.at[my_row, block],
-            dst_ref=gathered.at[my_row, block],
-            send_sem=send_row.at[peer],
-            recv_sem=recv_row.at[my_row],
-            device_id=(peer, my_col),
+            src_ref=gathered.at[my_row, my_inner, block],
+            dst_ref=gathered.at[my_row, my_inner, block],
+            send_sem=send_plane.at[row, place],
+            recv_sem=recv_plane.at[my_row, my_inner],
+            device_id=(row, my_outer * inner + place),
             device_id_type=MESH,
         )
 
-    for peer in col_peers:
-        col_copy(peer, my_col).start()
-    for peer in row_peers:
-        row_copy(my_col, peer).start()
-    for k in range(1, cols):
-        source = lax.rem(my_col + cols - k, cols)
-        pltpu.make_async_copy(
-            gathered.at[my_row, source], gathered.at[my_row, source], recv_col.at[source]
-        ).wait()
-        for peer in row_peers:
-            row_copy(source, peer).start()
-    for peer in row_peers:
-        pltpu.make_async_copy(gathered.at[peer], gathered.at[peer], recv_row.at[peer]).wait()
+    def arrived(ref, semaphore):
+        pltpu.make_async_copy(ref, ref, semaphore).wait()
+
+    for place in line[::-1]:
+        line_copy(place, my_outer).start()
+    for row, place in plane:
+        plane_copy(my_outer, row, place).start()
+    for source in line:
+        arrived(gathered.at[my_row, my_inner, source], recv_line.at[source])
+        for row, place in plane:
+            plane_copy(source, row, place).start()
+    for row, place in plane:
+        arrived(gathered.at[row, place], recv_plane.at[row, place])
 
     packed = gathered[...].reshape(particles, LANES)
     lane = lax.broadcasted_iota(jnp.int32, (1, LANES), 1)
@@ -109,13 +132,15 @@
         select.astype(f32).astype(bf16), packed, (((1,), (1,)), ((), ())), preferred_element_type=f32
     )
 
+    tiles = particles // LANES
+
     @pl.loop(0, particles // 16)
     def _(step):
         start = pl.multiple_of(step * 16, 16)
         at_rows = pl.ds(start, 16)
         row_pos = [pos_cols[at_rows, pl.ds(a * LANES, LANES)] for a in range(3)]
         row_label = start + lax.broadcasted_iota(jnp.int32, (16, LANES), 0)
-        for tile in range(particles // LANES):
+        for tile in range(tiles):
             at_cols = pl.ds(tile * LANES, LANES)
             d = [row_pos[a] - pos_rows[pl.ds(a * 16, 16), at_cols] for a in range(3)]
             col_label = tile * LANES + lax.broadcasted_iota(jnp.int32, (16, LANES), 1)
@@ -133,7 +158,7 @@
                 element = hd[a] * d[b]
                 if a == b:
                     element = element + f
-                mobility[at_rows, pl.ds(n * particles + tile * LANES, LANES)] = element.astype(bf16)
+                mobility[n * tiles + tile, at_rows, :] = element.astype(bf16)
 
     def set_weights(x):
         down = pltpu.roll(x, LANES - samples, 1)
@@ -158,8 +183,18 @@
         column = column + pltpu.roll(column, samples, 1)
         return column[0:1, :]
 
+    def couple():
+        half = particles // 2
+        parts = []
+        for start in (0, half):
+            chunk = jnp.concatenate(
+                [mobility[slab, pl.ds(start, half), :] for slab in range(6 * tiles)], axis=1
+            )
+            parts.append(jnp.dot(chunk, weights[...], preferred_element_type=f32))
+        return jnp.concatenate(parts, axis=0)
+
     is_noise = lane < 3 * samples
-    me = pl.multiple_of((my_row * cols + my_col) * per_device, per_device)
+    me = pl.multiple_of(((my_row * inner + my_inner) * outer + my_outer) * per_device, per_device)
     at_own = pl.ds(me, per_device)
     wide = packed.astype(f32)
     set_weights(wide)
@@ -169,7 +204,7 @@
     noise = noise_full[...]
     length = jnp.sqrt(total(noise * noise) + 1e-06)
     inverse = 1.0 / length
-    coupled = jnp.dot(mobility[...], weights[...], preferred_element_type=f32)
+    coupled = couple()
     basis_one = noise * inverse
     image_one = basis_one + coupled * inverse
     alpha_one = total(basis_one * image_one)
@@ -178,7 +213,7 @@
     basis_two = remainder * (1.0 / beta_one)
     image[...] = basis_two
     set_weights(basis_two)
-    coupled = jnp.dot(mobility[...], weights[...], preferred_element_type=f32)
+    coupled = couple()
     basis_two = image[...]
     alpha_two = total(basis_two * (basis_two + coupled))
     det_root = jnp.sqrt(alpha_one * alpha_two - beta_one * beta_one)
@@ -191,37 +226,39 @@
     for b in range(3):
         out_ref[b] = result[:, b * samples : (b + 1) * samples]
 
-    for peer in col_peers:
-        col_copy(peer, my_col).wait_send()
-    for peer in row_peers:
-        pltpu.make_async_copy(gathered.at[my_row], gathered.at[my_row], send_row.at[peer]).wait()
+    for place in line:
+        line_copy(place, my_outer).wait_send()
+    for row, place in plane:
+        arrived(gathered.at[my_row, my_inner], send_plane.at[row, place])
 
 
 def replicated(mesh, positions, thermal_noise):
     rows, cols = mesh.shape["row"], mesh.shape["col"]
     samples, _, per_device = thermal_noise.shape
     particles = rows * cols * per_device
+    inner = 2 if cols % 2 == 0 else 1
+    outer = cols // inner
     f32, bf16 = jnp.float32, jnp.bfloat16
     vmem = pl.BlockSpec(memory_space=pltpu.VMEM)
     out = pl.pallas_call(
-        functools.partial(replicated_kernel, rows, cols),
+        functools.partial(replicated_kernel, rows, outer, inner),
         out_shape=jax.ShapeDtypeStruct((3, per_device, samples), f32),
         in_specs=[vmem, vmem],
         out_specs=vmem,
         scratch_shapes=[
-            pltpu.VMEM((rows, cols, per_device, LANES), bf16),
+            pltpu.VMEM((rows, inner, outer, per_device, LANES), bf16),
             pltpu.VMEM((16, LANES), f32),
             pltpu.VMEM((per_device, LANES), f32),
             pltpu.VMEM((particles, LANES), f32),
             pltpu.VMEM((particles, 3 * LANES), f32),
             pltpu.VMEM((3 * 16, particles), f32),
-            pltpu.VMEM((particles, 6 * particles), bf16),
+            pltpu.VMEM((6 * particles // LANES, particles, LANES), bf16),
             pltpu.VMEM((6 * particles, LANES), bf16),
             pltpu.VMEM((particles, LANES), f32),
-            pltpu.SemaphoreType.DMA((cols,)),
-            pltpu.SemaphoreType.DMA((cols,)),
-            pltpu.SemaphoreType.DMA((rows,)),
-            pltpu.SemaphoreType.DMA((rows,)),
+            pltpu.SemaphoreType.DMA((outer,)),
+            pltpu.SemaphoreType.DMA((outer,)),
+            pltpu.SemaphoreType.DMA((rows, inner)),
+            pltpu.SemaphoreType.DMA((rows, inner)),
         ],
         compiler_params=pltpu.CompilerParams(collective_id=0, has_side_effects=True),
         name="lanczos",

time: 21.5 us -> 19.6 us (0.912)
  Pallas kernels: 19.9 us -> 18 us
    pallas_call x1, Pallas kernels: 19.9 us -> 18 us  [replicated(): pl.pallas_call(functools.partial(replicated_kernel, rows, outer, inner),...]
where the time goes in v2:
time: 19.6 us; the launch traced here: 19.4 us
  Pallas kernels  18 us (92%)
  local copies, waits for them, and re-layouts  1.35 us (7%)
    pallas_call x1, Pallas kernels, replicated(): pl.pallas_call(functools.partial(replicated_kernel, rows, outer, inner),...  18 us
    unnamed x1, local copies, waits for them, and re-layouts  1.35 us

profile of v2, /device:TPU:0, one launch (start us, length us, event | category | flops | bytes accessed | tf_op | source)
XLA Modules:
  0.0 19.4 jit_solution(15668636361121067487)
XLA Ops:
  0.0 18.0 %lanczos.1 = f32[3,16,32]{2,1,0:T(8,128)} custom-call(f32[3,16,32]{2,1,0:T(8,128)} %bitcast.3, f32[3,16]{1,0:T(4,128)} %pos_ref.1), custom_call_target="tpu_custom_call" | custom-call | tf_op jit(solution)/shard_map/lanczos/pallas_call | solution.py:243
  18.0 1.3 %copy.4 = f32[32,3,16]{0,2,1:T(8,128)} copy(f32[32,3,16]{0,2,1:T(8,128)} %bitcast.2) | data formatting | bytes 12288

commit v3 on v2

--- a/solution.py
+++ b/solution.py
@@ -13,8 +13,6 @@
 
 
 def partner(place, k, size):
-    if size & (size - 1):
-        return lax.rem(place + k, size)
     result = 0
     bit = 1
     while bit < size:
@@ -51,20 +49,19 @@
     my_row, my_col = lax.axis_index("row"), lax.axis_index("col")
 
     my_outer, my_inner = my_col // inner, lax.rem(my_col, inner)
-    line = [partner(my_outer, k, outer) for k in range(1, outer)]
+    line = [partner(my_outer, k, outer) for k in range(outer)]
     plane = [
         (partner(my_row, j, rows), partner(my_inner, i, inner))
         for i in range(inner)
         for j in range(rows)
-        if i or j
     ]
 
     barrier = pltpu.get_barrier_semaphore()
-    for place in line:
+    for place in line[1:]:
         pl.semaphore_signal(
             barrier, inc=1, device_id=(my_row, place * inner + my_inner), device_id_type=MESH
         )
-    for row, place in plane:
+    for row, place in plane[1:]:
         pl.semaphore_signal(
             barrier, inc=1, device_id=(row, my_outer * inner + place), device_id_type=MESH
         )
@@ -81,84 +78,104 @@
         own_ref[:, pl.ds(b * samples, samples)] = noise_ref[b]
     own_ref[:, pl.ds(3 * samples, 16)] = turned[0:per_device, :]
     own = own_ref[...]
-    gathered[my_row, my_inner, my_outer] = own.astype(bf16)
-
-    pl.semaphore_wait(barrier, len(line) + len(plane))
-
-    def line_copy(place, source):
+    gathered[0, 0] = own.astype(bf16)
+
+    pl.semaphore_wait(barrier, len(line) + len(plane) - 2)
+
+    def line_copy(k):
         return pltpu.make_async_remote_copy(
-            src_ref=gathered.at[my_row, my_inner, my_outer],
-            dst_ref=gathered.at[my_row, my_inner, my_outer],
-            send_sem=send_line.at[place],
-            recv_sem=recv_line.at[source],
-            device_id=(my_row, place * inner + my_inner),
+            src_ref=gathered.at[0, 0],
+            dst_ref=gathered.at[0, k],
+            send_sem=send_line.at[k],
+            recv_sem=recv_line.at[k],
+            device_id=(my_row, line[k] * inner + my_inner),
             device_id_type=MESH,
         )
 
-    def plane_copy(block, row, place):
+    def plane_copy(block, k):
         return pltpu.make_async_remote_copy(
-            src_ref=gathered.at[my_row, my_inner, block],
-            dst_ref=gathered.at[my_row, my_inner, block],
-            send_sem=send_plane.at[row, place],
-            recv_sem=recv_plane.at[my_row, my_inner],
-            device_id=(row, my_outer * inner + place),
+            src_ref=gathered.at[0, block],
+            dst_ref=gathered.at[k, block],
+            send_sem=send_plane.at[k],
+            recv_sem=recv_plane.at[k],
+            device_id=(plane[k][0], my_outer * inner + plane[k][1]),
             device_id_type=MESH,
         )
 
-    def arrived(ref, semaphore):
+    def finished(ref, semaphore):
         pltpu.make_async_copy(ref, ref, semaphore).wait()
 
-    for place in line[::-1]:
-        line_copy(place, my_outer).start()
-    for row, place in plane:
-        plane_copy(my_outer, row, place).start()
-    for source in line:
-        arrived(gathered.at[my_row, my_inner, source], recv_line.at[source])
-        for row, place in plane:
-            plane_copy(source, row, place).start()
-    for row, place in plane:
-        arrived(gathered.at[row, place], recv_plane.at[row, place])
-
-    packed = gathered[...].reshape(particles, LANES)
+    for k in range(outer - 1, 0, -1):
+        line_copy(k).start()
+    for k in range(1, len(plane)):
+        plane_copy(0, k).start()
+    for block in range(1, outer):
+        finished(gathered.at[0, block], recv_line.at[block])
+        for k in range(1, len(plane)):
+            plane_copy(block, k).start()
+
     lane = lax.broadcasted_iota(jnp.int32, (1, LANES), 1)
     field = lax.broadcasted_iota(jnp.int32, (LANES, 3 * LANES), 0) - 3 * samples
     target = lax.broadcasted_iota(jnp.int32, (LANES, 3 * LANES), 1) // LANES
     select = (field == target) | (field == target + 3) | (field == target + 6)
-    pos_cols[...] = jnp.dot(packed, select.astype(f32).astype(bf16), preferred_element_type=f32)
+    over_lanes = select.astype(f32).astype(bf16)
     field = lax.broadcasted_iota(jnp.int32, (3 * 16, LANES), 1) - 3 * samples
     target = lax.broadcasted_iota(jnp.int32, (3 * 16, LANES), 0) // 16
     select = (field == target) | (field == target + 3) | (field == target + 6)
-    pos_rows[...] = lax.dot_general(
-        select.astype(f32).astype(bf16), packed, (((1,), (1,)), ((), ())), preferred_element_type=f32
-    )
-
+    over_rows = select.astype(f32).astype(bf16)
     tiles = particles // LANES
 
-    @pl.loop(0, particles // 16)
-    def _(step):
-        start = pl.multiple_of(step * 16, 16)
+    def form(start, tile, on_diagonal):
         at_rows = pl.ds(start, 16)
-        row_pos = [pos_cols[at_rows, pl.ds(a * LANES, LANES)] for a in range(3)]
-        row_label = start + lax.broadcasted_iota(jnp.int32, (16, LANES), 0)
-        for tile in range(tiles):
-            at_cols = pl.ds(tile * LANES, LANES)
-            d = [row_pos[a] - pos_rows[pl.ds(a * 16, 16), at_cols] for a in range(3)]
+        d = [
+            pos_cols[at_rows, pl.ds(a * LANES, LANES)]
+            - pos_rows[pl.ds(a * 16, 16), pl.ds(tile * LANES, LANES)]
+            for a in range(3)
+        ]
+        q = d[0] * d[0] + d[1] * d[1] + d[2] * d[2]
+        if on_diagonal:
+            row_label = start + lax.broadcasted_iota(jnp.int32, (16, LANES), 0)
             col_label = tile * LANES + lax.broadcasted_iota(jnp.int32, (16, LANES), 1)
             retain = row_label != col_label
-            q = jnp.where(retain, d[0] * d[0] + d[1] * d[1] + d[2] * d[2], 4.0)
-            u = lax.rsqrt(q)
-            r = q * u
-            near = r < 2.0
-            u2 = u * u
-            f = jnp.where(near, 1.0 - 0.28125 * r, u * (0.75 + 0.5 * u2))
+            q = jnp.where(retain, q, 4.0)
+        u = lax.rsqrt(q)
+        r = q * u
+        near = r < 2.0
+        u2 = u * u
+        f = jnp.where(near, 1.0 - 0.28125 * r, u * (0.75 + 0.5 * u2))
+        if on_diagonal:
             f = jnp.where(retain, f, 0.0)
-            h = u * jnp.where(near, 0.09375, u2 * (0.75 - 1.5 * u2))
-            hd = [h * d[a] for a in range(3)]
-            for n, (a, b) in enumerate(BLOCKS):
-                element = hd[a] * d[b]
-                if a == b:
-                    element = element + f
-                mobility[n * tiles + tile, at_rows, :] = element.astype(bf16)
+        h = u * jnp.where(near, 0.09375, u2 * (0.75 - 1.5 * u2))
+        hd = [h * d[a] for a in range(3)]
+        for n, (a, b) in enumerate(BLOCKS):
+            element = hd[a] * d[b]
+            if a == b:
+                element = element + f
+            mobility[n * tiles + tile, at_rows, :] = element.astype(bf16)
+
+    per_tile = LANES // (outer * per_device)
+    for tile in range(tiles):
+        for k in range(tile * per_tile, (tile + 1) * per_tile):
+            if k:
+                finished(gathered.at[k], recv_plane.at[k])
+        packed = gathered[pl.ds(tile * per_tile, per_tile)].reshape(LANES, LANES)
+        pos_cols[pl.ds(tile * LANES, LANES), :] = jnp.dot(
+            packed, over_lanes, preferred_element_type=f32
+        )
+        pos_rows[:, pl.ds(tile * LANES, LANES)] = lax.dot_general(
+            over_rows, packed, (((1,), (1,)), ((), ())), preferred_element_type=f32
+        )
+
+        @pl.loop(0, LANES // 16)
+        def _(step, tile=tile):
+            for other in range(tile + 1):
+                start = pl.multiple_of(tile * LANES + step * 16, 16)
+                form(start, other, other == tile)
+            for other in range(tile):
+                start = pl.multiple_of(other * LANES + step * 16, 16)
+                form(start, tile, False)
+
+    packed = gathered[...].reshape(particles, LANES)
 
     def set_weights(x):
         down = pltpu.roll(x, LANES - samples, 1)
@@ -194,8 +211,7 @@
         return jnp.concatenate(parts, axis=0)
 
     is_noise = lane < 3 * samples
-    me = pl.multiple_of(((my_row * inner + my_inner) * outer + my_outer) * per_device, per_device)
-    at_own = pl.ds(me, per_device)
+    at_own = pl.ds(0, per_device)
     wide = packed.astype(f32)
     set_weights(wide)
     noise_full[...] = jnp.where(is_noise, wide, 0.0)
@@ -226,10 +242,10 @@
     for b in range(3):
         out_ref[b] = result[:, b * samples : (b + 1) * samples]
 
-    for place in line:
-        line_copy(place, my_outer).wait_send()
-    for row, place in plane:
-        arrived(gathered.at[my_row, my_inner], send_plane.at[row, place])
+    for k in range(1, outer):
+        line_copy(k).wait_send()
+    for k in range(1, len(plane)):
+        finished(gathered.at[0], send_plane.at[k])
 
 
 def replicated(mesh, positions, thermal_noise):
@@ -246,7 +262,7 @@
         in_specs=[vmem, vmem],
         out_specs=vmem,
         scratch_shapes=[
-            pltpu.VMEM((rows, inner, outer, per_device, LANES), bf16),
+            pltpu.VMEM((rows * inner, outer, per_device, LANES), bf16),
             pltpu.VMEM((16, LANES), f32),
             pltpu.VMEM((per_device, LANES), f32),
             pltpu.VMEM((particles, LANES), f32),
@@ -257,8 +273,8 @@
             pltpu.VMEM((particles, LANES), f32),
             pltpu.SemaphoreType.DMA((outer,)),
             pltpu.SemaphoreType.DMA((outer,)),
-            pltpu.SemaphoreType.DMA((rows, inner)),
-            pltpu.SemaphoreType.DMA((rows, inner)),
+            pltpu.SemaphoreType.DMA((rows * inner,)),
+            pltpu.SemaphoreType.DMA((rows * inner,)),
         ],
         compiler_params=pltpu.CompilerParams(collective_id=0, has_side_effects=True),
         name="lanczos",
@@ -267,13 +283,17 @@
 
 
 def fits(mesh, positions, thermal_noise):
-    devices = mesh.shape["row"] * mesh.shape["col"]
+    rows, cols = mesh.shape["row"], mesh.shape["col"]
     samples, _, particles = thermal_noise.shape
-    per_device = particles // devices
+    per_device = particles // (rows * cols)
+    outer = cols // 2 if cols % 2 == 0 else cols
     return (
-        4 * samples == LANES
+        rows & (rows - 1) == 0
+        and cols & (cols - 1) == 0
+        and 4 * samples == LANES
         and per_device % 16 == 0
-        and particles % LANES == 0
+        and LANES % (outer * per_device) == 0
+        and particles % (2 * LANES) == 0
         and 12 * particles * particles <= 2**24
     )
 

time: 19.6 us -> 19.3 us (0.985)
  Pallas kernels: 18 us -> 17.7 us
    pallas_call x1, Pallas kernels: 18 us -> 17.7 us  [replicated(): pl.pallas_call(functools.partial(replicated_kernel, rows, outer, inner),...]
where the time goes in v3:
time: 19.3 us; the launch traced here: 19 us
  Pallas kernels  17.7 us (92%)
  local copies, waits for them, and re-layouts  1.35 us (7%)
    pallas_call x1, Pallas kernels, replicated(): pl.pallas_call(functools.partial(replicated_kernel, rows, outer, inner),...  17.7 us
    unnamed x1, local copies, waits for them, and re-layouts  1.35 us

profile of v3, /device:TPU:0, one launch (start us, length us, event | category | flops | bytes accessed | tf_op | source)
XLA Modules:
  0.0 19.0 jit_solution(64575739406877294)
XLA Ops:
  0.0 17.7 %lanczos.1 = f32[3,16,32]{2,1,0:T(8,128)} custom-call(f32[3,16,32]{2,1,0:T(8,128)} %bitcast.3, f32[3,16]{1,0:T(4,128)} %pos_ref.1), custom_call_target="tpu_custom_call" | custom-call | tf_op jit(solution)/shard_map/lanczos/pallas_call | solution.py:259
  17.7 1.3 %copy.4 = f32[32,3,16]{0,2,1:T(8,128)} copy(f32[32,3,16]{0,2,1:T(8,128)} %bitcast.2) | data formatting | bytes 12288

commit v4 on v3

--- a/solution.py
+++ b/solution.py
@@ -175,13 +175,12 @@
                 start = pl.multiple_of(other * LANES + step * 16, 16)
                 form(start, tile, False)
 
-    packed = gathered[...].reshape(particles, LANES)
-
-    def set_weights(x):
+    group = lane // samples
+
+    def set_weights(start, x):
         down = pltpu.roll(x, LANES - samples, 1)
         up = pltpu.roll(x, samples, 1)
         across = pltpu.roll(x, 2 * samples, 1)
-        group = lane // samples
         moved = {
             (0, 0): jnp.where(group == 0, x, 0.0),
             (1, 1): jnp.where(group == 1, x, 0.0),
@@ -191,54 +190,98 @@
             (0, 2): jnp.where((group == 0) | (group == 2), across, 0.0),
         }
         for n, pair in enumerate(BLOCKS):
-            weights[pl.ds(n * particles, particles), :] = moved[pair].astype(bf16)
+            weights[pl.ds(n * particles + start, x.shape[0]), :] = moved[pair].astype(bf16)
+
+    def fold(x):
+        return jnp.sum(x.reshape(-1, 8, LANES), axis=0)
 
     def total(x):
-        column = jnp.sum(x, axis=0, keepdims=True)
-        column = jnp.broadcast_to(column, (8, LANES))
-        column = column + pltpu.roll(column, 2 * samples, 1)
-        column = column + pltpu.roll(column, samples, 1)
-        return column[0:1, :]
-
-    def couple():
-        half = particles // 2
-        parts = []
-        for start in (0, half):
-            chunk = jnp.concatenate(
-                [mobility[slab, pl.ds(start, half), :] for slab in range(6 * tiles)], axis=1
-            )
-            parts.append(jnp.dot(chunk, weights[...], preferred_element_type=f32))
-        return jnp.concatenate(parts, axis=0)
+        row = jnp.broadcast_to(jnp.sum(x, axis=0, keepdims=True), (8, LANES))
+        row = row + pltpu.roll(row, 2 * samples, 1)
+        row = row + pltpu.roll(row, samples, 1)
+        return row[0:1, :]
+
+    step_rows = 64
+
+    def sweep(function):
+        def step(index, partial):
+            start = index * step_rows
+            return partial + function(start, pl.ds(start, step_rows))
+
+        partial = jnp.zeros((8, LANES), f32)
+        for index in range(particles // step_rows):
+            partial = step(index, partial)
+        return total(partial)
+
+    def product(row_tiles, col_tiles):
+        at_rows = pl.ds(row_tiles[0] * LANES, len(row_tiles) * LANES)
+        first, count = col_tiles[0], len(col_tiles)
+        left = jnp.concatenate(
+            [mobility[n * tiles + first + t, at_rows, :] for n in range(6) for t in range(count)],
+            axis=1,
+        )
+        right = jnp.concatenate(
+            [
+                weights[pl.ds(n * particles + first * LANES, count * LANES), :]
+                for n in range(6)
+            ],
+            axis=0,
+        )
+        return jnp.dot(left, right, preferred_element_type=f32)
 
     is_noise = lane < 3 * samples
     at_own = pl.ds(0, per_device)
-    wide = packed.astype(f32)
-    set_weights(wide)
-    noise_full[...] = jnp.where(is_noise, wide, 0.0)
+    low, high = list(range(tiles // 2)), list(range(tiles // 2, tiles))
+    at_low, at_high = pl.ds(0, particles // 2), pl.ds(particles // 2, particles // 2)
+    for tile in range(tiles):
+        wide = gathered[pl.ds(tile * per_tile, per_tile)].reshape(LANES, LANES).astype(f32)
+        noise_full[pl.ds(tile * LANES, LANES), :] = jnp.where(is_noise, wide, 0.0)
+        set_weights(tile * LANES, wide)
     noise_full[at_own, :] = jnp.where(is_noise, own_ref[...], 0.0)
 
-    noise = noise_full[...]
-    length = jnp.sqrt(total(noise * noise) + 1e-06)
+    def noise_square(start, at):
+        return fold(noise_full[at, :] * noise_full[at, :])
+
+    length = jnp.sqrt(sweep(noise_square) + 1e-06)
     inverse = 1.0 / length
-    coupled = couple()
-    basis_one = noise * inverse
-    image_one = basis_one + coupled * inverse
-    alpha_one = total(basis_one * image_one)
-    remainder = image_one - alpha_one * basis_one
-    beta_one = jnp.sqrt(total(remainder * remainder) + 1e-06)
-    basis_two = remainder * (1.0 / beta_one)
-    image[...] = basis_two
-    set_weights(basis_two)
-    coupled = couple()
-    basis_two = image[...]
-    alpha_two = total(basis_two * (basis_two + coupled))
+    image[at_low, :] = product(low, low + high)
+    image[at_high, :] = product(high, low + high)
+
+
+    def first_quotient(start, at):
+        basis_one = noise_full[at, :] * inverse
+        image_one = basis_one + image[at, :] * inverse
+        noise_full[at, :] = basis_one
+        image[at, :] = image_one
+        return fold(basis_one * image_one)
+
+    alpha_one = sweep(first_quotient)
+
+    def remainder_square(start, at):
+        remainder = image[at, :] - alpha_one * noise_full[at, :]
+        image[at, :] = remainder
+        return fold(remainder * remainder)
+
+    beta_one = jnp.sqrt(sweep(remainder_square) + 1e-06)
+    inverse_beta = 1.0 / beta_one
+
+    def second_basis(start, at):
+        basis_two = image[at, :] * inverse_beta
+        image[at, :] = basis_two
+        set_weights(start, basis_two)
+        return fold(basis_two * basis_two)
+
+    alpha_two = sweep(second_basis)
+    alpha_two = alpha_two + total(
+        fold(image[at_low, :] * product(low, low))
+        + 2.0 * fold(image[at_low, :] * product(low, high))
+        + fold(image[at_high, :] * product(high, high))
+    )
     det_root = jnp.sqrt(alpha_one * alpha_two - beta_one * beta_one)
     trace_root = jnp.sqrt(alpha_one + alpha_two + 2.0 * det_root)
     weight_one = (alpha_one + det_root) / trace_root
     weight_two = beta_one / trace_root
-    own_one = noise_full[at_own, :] * inverse
-    own_two = image[at_own, :]
-    result = 0.5 * length * (weight_one * own_one + weight_two * own_two)
+    result = 0.5 * length * (weight_one * noise_full[at_own, :] + weight_two * image[at_own, :])
     for b in range(3):
         out_ref[b] = result[:, b * samples : (b + 1) * samples]
 

time: 19.3 us -> 19.1 us (0.990)
  Pallas kernels: 17.7 us -> 17.5 us
    pallas_call x1, Pallas kernels: 17.7 us -> 17.5 us  [replicated(): pl.pallas_call(functools.partial(replicated_kernel, rows, outer, inner),...]
where the time goes in v4:
time: 19.1 us; the launch traced here: 18.8 us
  Pallas kernels  17.5 us (92%)
  local copies, waits for them, and re-layouts  1.35 us (7%)
    pallas_call x1, Pallas kernels, replicated(): pl.pallas_call(functools.partial(replicated_kernel, rows, outer, inner),...  17.5 us
    unnamed x1, local copies, waits for them, and re-layouts  1.35 us

profile of v4, /device:TPU:0, one launch (start us, length us, event | category | flops | bytes accessed | tf_op | source)
XLA Modules:
  0.0 18.8 jit_solution(12910842061404334267)
XLA Ops:
  0.0 17.5 %lanczos.1 = f32[3,16,32]{2,1,0:T(8,128)} custom-call(f32[3,16,32]{2,1,0:T(8,128)} %bitcast.3, f32[3,16]{1,0:T(4,128)} %pos_ref.1), custom_call_target="tpu_custom_call" | custom-call | tf_op jit(solution)/shard_map/lanczos/pallas_call | solution.py:302
  17.5 1.3 %copy.4 = f32[32,3,16]{0,2,1:T(8,128)} copy(f32[32,3,16]{0,2,1:T(8,128)} %bitcast.2) | data formatting | bytes 12288

commit v5 on v4

--- a/solution.py
+++ b/solution.py
@@ -153,28 +153,6 @@
                 element = element + f
             mobility[n * tiles + tile, at_rows, :] = element.astype(bf16)
 
-    per_tile = LANES // (outer * per_device)
-    for tile in range(tiles):
-        for k in range(tile * per_tile, (tile + 1) * per_tile):
-            if k:
-                finished(gathered.at[k], recv_plane.at[k])
-        packed = gathered[pl.ds(tile * per_tile, per_tile)].reshape(LANES, LANES)
-        pos_cols[pl.ds(tile * LANES, LANES), :] = jnp.dot(
-            packed, over_lanes, preferred_element_type=f32
-        )
-        pos_rows[:, pl.ds(tile * LANES, LANES)] = lax.dot_general(
-            over_rows, packed, (((1,), (1,)), ((), ())), preferred_element_type=f32
-        )
-
-        @pl.loop(0, LANES // 16)
-        def _(step, tile=tile):
-            for other in range(tile + 1):
-                start = pl.multiple_of(tile * LANES + step * 16, 16)
-                form(start, other, other == tile)
-            for other in range(tile):
-                start = pl.multiple_of(other * LANES + step * 16, 16)
-                form(start, tile, False)
-
     group = lane // samples
 
     def set_weights(start, x):
@@ -232,11 +210,44 @@
     is_noise = lane < 3 * samples
     at_own = pl.ds(0, per_device)
     low, high = list(range(tiles // 2)), list(range(tiles // 2, tiles))
+    early, late = list(range(tiles // 2)), list(range(tiles // 2, tiles))
     at_low, at_high = pl.ds(0, particles // 2), pl.ds(particles // 2, particles // 2)
+    at_early, at_late = pl.ds(0, len(early) * LANES), pl.ds(len(early) * LANES, len(late) * LANES)
+    per_tile = LANES // (outer * per_device)
     for tile in range(tiles):
-        wide = gathered[pl.ds(tile * per_tile, per_tile)].reshape(LANES, LANES).astype(f32)
+        for k in range(tile * per_tile, (tile + 1) * per_tile):
+            if k:
+                finished(gathered.at[k], recv_plane.at[k])
+        packed = gathered[pl.ds(tile * per_tile, per_tile)].reshape(LANES, LANES)
+        pos_cols[pl.ds(tile * LANES, LANES), :] = jnp.dot(
+            packed, over_lanes, preferred_element_type=f32
+        )
+        pos_rows[:, pl.ds(tile * LANES, LANES)] = lax.dot_general(
+            over_rows, packed, (((1,), (1,)), ((), ())), preferred_element_type=f32
+        )
+
+        wide = packed.astype(f32)
         noise_full[pl.ds(tile * LANES, LANES), :] = jnp.where(is_noise, wide, 0.0)
         set_weights(tile * LANES, wide)
+
+        if tile == tiles - 1:
+            image[pl.ds(0, len(early) * LANES), :] = product(early, low)
+            for step in range(LANES // 16):
+                for other in range(tile + 1):
+                    form(tile * LANES + step * 16, other, other == tile)
+                for other in range(tile):
+                    form(other * LANES + step * 16, tile, False)
+        else:
+
+            @pl.loop(0, LANES // 16)
+            def _(step, tile=tile):
+                for other in range(tile + 1):
+                    start = pl.multiple_of(tile * LANES + step * 16, 16)
+                    form(start, other, other == tile)
+                for other in range(tile):
+                    start = pl.multiple_of(other * LANES + step * 16, 16)
+                    form(start, tile, False)
+
     noise_full[at_own, :] = jnp.where(is_noise, own_ref[...], 0.0)
 
     def noise_square(start, at):
@@ -244,9 +255,8 @@
 
     length = jnp.sqrt(sweep(noise_square) + 1e-06)
     inverse = 1.0 / length
-    image[at_low, :] = product(low, low + high)
-    image[at_high, :] = product(high, low + high)
-
+    image[at_early, :] = image[at_early, :] + product(early, high)
+    image[at_late, :] = product(late, low + high)
 
     def first_quotient(start, at):
         basis_one = noise_full[at, :] * inverse

time: 19.1 us -> 18.7 us (0.979)
  Pallas kernels: 17.5 us -> 17.1 us
    pallas_call x1, Pallas kernels: 17.5 us -> 17.1 us  [replicated(): pl.pallas_call(functools.partial(replicated_kernel, rows, outer, inner),...]
where the time goes in v5:
time: 18.7 us; the launch traced here: 18.5 us
  Pallas kernels  17.1 us (91%)
  local copies, waits for them, and re-layouts  1.35 us (7%)
    pallas_call x1, Pallas kernels, replicated(): pl.pallas_call(functools.partial(replicated_kernel, rows, outer, inner),...  17.1 us
    unnamed x1, local copies, waits for them, and re-layouts  1.35 us

profile of v5, /device:TPU:0, one launch (start us, length us, event | category | flops | bytes accessed | tf_op | source)
XLA Modules:
  0.0 18.5 jit_solution(5761412265212178367)
XLA Ops:
  0.0 17.1 %lanczos.1 = f32[3,16,32]{2,1,0:T(8,128)} custom-call(f32[3,16,32]{2,1,0:T(8,128)} %bitcast.3, f32[3,16]{1,0:T(4,128)} %pos_ref.1), custom_call_target="tpu_custom_call" | custom-call | tf_op jit(solution)/shard_map/lanczos/pallas_call | solution.py:312
  17.1 1.3 %copy.4 = f32[32,3,16]{0,2,1:T(8,128)} copy(f32[32,3,16]{0,2,1:T(8,128)} %bitcast.2) | data formatting | bytes 12288
